TPU v7x, 256 devices: a whole 4x4x8 slice. The times are simulated.
256 devices in a mesh: tm: 16 (over x, y_lo, core), space: 16 (over y_hi, z).
Axes of the slice: x: 4, y: 4 (y_hi: 2, y_lo: 2; y = y_hi * 2 + y_lo), z: 8, core: 2. Of those that a mesh axis runs over, the one named last changes fastest.
Arguments:
- snapshots: bfloat16 [8192, 32768], P('tm', 'space'), may hold values from -6 to 6
- outlier_cols: int32 [64, 64], P('tm', 'space'), may hold values from 0 to 15
- outlier_values: bfloat16 [64, 64, 128, 128], P('tm', 'space'), may hold values from -12 to 12
- threshold: float32 [], replicated, may hold values from 0.3 to 0.9
Outputs:
- gram_band: float32 [8192, 9, 512], P('tm', None, 'space')
Inputs may be any that keep to these rules, and one draw needn't show every extreme that they name: `outlier_cols`: entry k of a row lies in the points of space block k // 4; repeated entries add.
All inputs are finite; a program needn't handle non-finite values.
Results may differ from a plain program's by a relative error of at most 0.0021.
Values may be sent and summed in bfloat16 or wider, within the bound.
A program may use at most 128 MiB of HBM per device.

v0:
```python
import jax
import jax.numpy as jnp
from jax import lax
from jax.sharding import PartitionSpec as P

ST = 128


def passed_along(x, axis, by):
    size = lax.axis_size(axis)
    return lax.ppermute(x, axis, [(i, (i + by) % size) for i in range(size)])


def tile_product(own, other):
    return lax.dot_general(own, other, (((1,), (1,)), ((), ())), preferred_element_type=jnp.float32)


def local(snapshots, outlier_cols, outlier_values, threshold):
    block_rows, points = snapshots.shape
    tiles_dev = points // ST
    n_loop = lax.axis_size("tm")
    half = n_loop // 2
    onehot = (
        outlier_cols[:, :, None] == jnp.arange(tiles_dev, dtype=jnp.int32)[None, None, :]
    ).astype(jnp.bfloat16)
    dense = jnp.einsum("rkos,rkn->rons", outlier_values, onehot, preferred_element_type=jnp.float32)
    dense = dense.reshape(block_rows, points)
    diff = snapshots.astype(jnp.float32) - dense
    cleaned = (jnp.sign(diff) * jnp.maximum(jnp.abs(diff) - threshold, 0.0)).astype(jnp.bfloat16)
    scale = 1.0 / jnp.sqrt(jnp.float32(points * lax.axis_size("space")))
    kept = []

    def finish(term):
        kept.append(term)

    finish(tile_product(cleaned, cleaned))
    moving = cleaned
    for step in range(half):
        moving = passed_along(moving, "tm", -1)
        finish(tile_product(cleaned, moving))
    band = lax.psum_scatter(jnp.stack(kept, axis=1), "space", scatter_dimension=2, tiled=True)
    return band * scale


def solution(mesh):
    placed = (P("tm", "space"), P("tm", "space"), P("tm", "space", None, None), P())
    return jax.shard_map(
        local, mesh=mesh, in_specs=placed, out_specs=P("tm", None, "space"), check_vma=False
    )
```

profile of v0, /device:TPU:2, one launch (start us, length us, event | category | flops | bytes accessed | tf_op | source)
XLA Modules:
  0.0 548.5 jit_solution(18085181693283728398)
XLA Ops:
  9.5 2.5 multiply_convert_fusion
  13.0 23.6 %collective-permute-done = bf16[512,2048]{1,0:T(8,128)(2,1)S(1)} collective-permute-done((bf16[512,2048]{1,0:T(8,128)(2,1)S(1)}, bf16[512,2048]{1,0:T(8,128)(2,1)S(1)}, u32[]{:S(2)}, u32[]{:S(2)}) %collective-permute-start) | collective-permute-done | bytes 2097184 | tf_op jit(solution)/shard_map/ppermute | solution.py:11
  36.6 2.8 collective-permute-start.1
  39.4 23.6 %collective-permute-done.1 = bf16[512,2048]{1,0:T(8,128)(2,1)S(1)} collective-permute-done((bf16[512,2048]{1,0:T(8,128)(2,1)S(1)}, bf16[512,2048]{1,0:T(8,128)(2,1)S(1)}, u32[]{:S(2)}, u32[]{:S(2)}) %collective-permute-start.1) | collective-permute-done | bytes 2097184 | tf_op jit(solution)/shard_map/ppermute | solution.py:11
  63.0 2.8 collective-permute-start.2
  65.8 23.6 %collective-permute-done.2 = bf16[512,2048]{1,0:T(8,128)(2,1)S(1)} collective-permute-done((bf16[512,2048]{1,0:T(8,128)(2,1)S(1)}, bf16[512,2048]{1,0:T(8,128)(2,1)S(1)}, u32[]{:S(2)}, u32[]{:S(2)}) %collective-permute-start.2) | collective-permute-done | bytes 2097184 | tf_op jit(solution)/shard_map/ppermute | solution.py:11
  89.3 2.8 collective-permute-start.3
  92.1 23.6 %collective-permute-done.3 = bf16[512,2048]{1,0:T(8,128)(2,1)S(1)} collective-permute-done((bf16[512,2048]{1,0:T(8,128)(2,1)S(1)}, bf16[512,2048]{1,0:T(8,128)(2,1)S(1)}, u32[]{:S(2)}, u32[]{:S(2)}) %collective-permute-start.3) | collective-permute-done | bytes 2097184 | tf_op jit(solution)/shard_map/ppermute | solution.py:11
  115.7 2.8 collective-permute-start.4
  118.5 23.6 %collective-permute-done.4 = bf16[512,2048]{1,0:T(8,128)(2,1)S(1)} collective-permute-done((bf16[512,2048]{1,0:T(8,128)(2,1)S(1)}, bf16[512,2048]{1,0:T(8,128)(2,1)S(1)}, u32[]{:S(2)}, u32[]{:S(2)}) %collective-permute-start.4) | collective-permute-done | bytes 2097184 | tf_op jit(solution)/shard_map/ppermute | solution.py:11
  142.0 2.8 collective-permute-start.5
  144.8 23.6 %collective-permute-done.5 = bf16[512,2048]{1,0:T(8,128)(2,1)S(1)} collective-permute-done((bf16[512,2048]{1,0:T(8,128)(2,1)S(1)}, bf16[512,2048]{1,0:T(8,128)(2,1)S(1)}, u32[]{:S(2)}, u32[]{:S(2)}) %collective-permute-start.5) | collective-permute-done | bytes 2097184 | tf_op jit(solution)/shard_map/ppermute | solution.py:11
  168.4 2.8 collective-permute-start.6
  173.5 2.3 fusion.7
  175.8 19.0 %collective-permute-done.6 = bf16[512,2048]{1,0:T(8,128)(2,1)S(1)} collective-permute-done((bf16[512,2048]{1,0:T(8,128)(2,1)S(1)}, bf16[512,2048]{1,0:T(8,128)(2,1)S(1)}, u32[]{:S(2)}, u32[]{:S(2)}) %collective-permute-start.6) | collective-permute-done | bytes 2097184 | tf_op jit(solution)/shard_map/ppermute | solution.py:11
  194.7 2.8 collective-permute-start.7
  204.4 2.3 fusion.3
  206.7 2.3 fusion.2
  209.0 2.3 fusion.1
  211.3 9.8 %collective-permute-done.7 = bf16[512,2048]{1,0:T(8,128)(2,1)S(1)} collective-permute-done((bf16[512,2048]{1,0:T(8,128)(2,1)S(1)}, bf16[512,2048]{1,0:T(8,128)(2,1)S(1)}, u32[]{:S(2)}, u32[]{:S(2)}) %collective-permute-start.7) | collective-permute-done | bytes 2097184 | tf_op jit(solution)/shard_map/ppermute | solution.py:11
  221.1 2.4 fusion
  223.5 16.7 %copy.11 = f32[512,9,512]{0,1,2:T(8,128)} copy(f32[512,9,512]{2,0,1:T(8,128)} %fusion) | data formatting | bytes 18874368 | tf_op jit(solution)/shard_map/stack | solution.py:41
  240.2 299.0 %reduce-scatter.2.cloned.1.call-done = f32[512,9,32]{0,1,2:T(8,128)} async-done(((f32[512,9,512]{0,1,2:T(8,128)}), f32[512,9,32]{0,1,2:T(8,128)}) %reduce-scatter.2.cloned.1.call-update) | async-done | bytes 589840 | tf_op jit(solution)/shard_map/reduce_scatter | solution.py:41
  539.2 2.4 copy_multiply_fusion
  (12 shorter events, 12.4 us)
Async XLA Ops:
  6.5 1.1 copy-start
  6.5 532.7 %reduce-scatter.2.cloned.1.call-start = ((), (), s32[]{:S(2)}) async-start(), calls=%async_computation.1 | async-start | bytes 17825792 | tf_op jit(solution)/shard_map/reduce_scatter | solution.py:41
  7.6 1.9 copy-start.1
  12.0 24.6 %collective-permute-start = (bf16[512,2048]{1,0:T(8,128)(2,1)S(1)}, bf16[512,2048]{1,0:T(8,128)(2,1)S(1)}, u32[]{:S(2)}, u32[]{:S(2)}) collective-permute-start(bf16[512,2048]{1,0:T(8,128)(2,1)S(1)} %multiply_convert_fusion), channel_id=1, source_target_pairs={{0,240},{16,0},{32,16},{48,32},{64,48},{80,64},{96,80},{112,96},{1... | collective-permute-start | bytes 6291464 | tf_op jit(solution)/shard_map/ppermute | solution.py:11
  36.6 26.4 %collective-permute-start.1 = (bf16[512,2048]{1,0:T(8,128)(2,1)S(1)}, bf16[512,2048]{1,0:T(8,128)(2,1)S(1)}, u32[]{:S(2)}, u32[]{:S(2)}) collective-permute-start(bf16[512,2048]{1,0:T(8,128)(2,1)S(1)} %collective-permute-done), channel_id=1, source_target_pairs={{0,240},{16,0},{32,16},{48,32},{64,48},{80,64},{96,80},{112,96},{1... | collective-permute-start | bytes 6291464 | tf_op jit(solution)/shard_map/ppermute | solution.py:11
  63.0 26.4 %collective-permute-start.2 = (bf16[512,2048]{1,0:T(8,128)(2,1)S(1)}, bf16[512,2048]{1,0:T(8,128)(2,1)S(1)}, u32[]{:S(2)}, u32[]{:S(2)}) collective-permute-start(bf16[512,2048]{1,0:T(8,128)(2,1)S(1)} %collective-permute-done.1), channel_id=1, source_target_pairs={{0,240},{16,0},{32,16},{48,32},{64,48},{80,64},{96,80},{112,96},{1... | collective-permute-start | bytes 6291464 | tf_op jit(solution)/shard_map/ppermute | solution.py:11
  89.3 26.4 %collective-permute-start.3 = (bf16[512,2048]{1,0:T(8,128)(2,1)S(1)}, bf16[512,2048]{1,0:T(8,128)(2,1)S(1)}, u32[]{:S(2)}, u32[]{:S(2)}) collective-permute-start(bf16[512,2048]{1,0:T(8,128)(2,1)S(1)} %collective-permute-done.2), channel_id=1, source_target_pairs={{0,240},{16,0},{32,16},{48,32},{64,48},{80,64},{96,80},{112,96},{1... | collective-permute-start | bytes 6291464 | tf_op jit(solution)/shard_map/ppermute | solution.py:11
  115.7 26.4 %collective-permute-start.4 = (bf16[512,2048]{1,0:T(8,128)(2,1)S(1)}, bf16[512,2048]{1,0:T(8,128)(2,1)S(1)}, u32[]{:S(2)}, u32[]{:S(2)}) collective-permute-start(bf16[512,2048]{1,0:T(8,128)(2,1)S(1)} %collective-permute-done.3), channel_id=1, source_target_pairs={{0,240},{16,0},{32,16},{48,32},{64,48},{80,64},{96,80},{112,96},{1... | collective-permute-start | bytes 6291464 | tf_op jit(solution)/shard_map/ppermute | solution.py:11
  142.0 26.4 %collective-permute-start.5 = (bf16[512,2048]{1,0:T(8,128)(2,1)S(1)}, bf16[512,2048]{1,0:T(8,128)(2,1)S(1)}, u32[]{:S(2)}, u32[]{:S(2)}) collective-permute-start(bf16[512,2048]{1,0:T(8,128)(2,1)S(1)} %collective-permute-done.4), channel_id=1, source_target_pairs={{0,240},{16,0},{32,16},{48,32},{64,48},{80,64},{96,80},{112,96},{1... | collective-permute-start | bytes 6291464 | tf_op jit(solution)/shard_map/ppermute | solution.py:11
  168.4 26.4 %collective-permute-start.6 = (bf16[512,2048]{1,0:T(8,128)(2,1)S(1)}, bf16[512,2048]{1,0:T(8,128)(2,1)S(1)}, u32[]{:S(2)}, u32[]{:S(2)}) collective-permute-start(bf16[512,2048]{1,0:T(8,128)(2,1)S(1)} %collective-permute-done.5), channel_id=1, source_target_pairs={{0,240},{16,0},{32,16},{48,32},{64,48},{80,64},{96,80},{112,96},{1... | collective-permute-start | bytes 6291464 | tf_op jit(solution)/shard_map/ppermute | solution.py:11
  194.7 26.4 %collective-permute-start.7 = (bf16[512,2048]{1,0:T(8,128)(2,1)S(1)}, bf16[512,2048]{1,0:T(8,128)(2,1)S(1)}, u32[]{:S(2)}, u32[]{:S(2)}) collective-permute-start(bf16[512,2048]{1,0:T(8,128)(2,1)S(1)} %collective-permute-done.6), channel_id=1, source_target_pairs={{0,240},{16,0},{32,16},{48,32},{64,48},{80,64},{96,80},{112,96},{1... | collective-permute-start | bytes 6291464 | tf_op jit(solution)/shard_map/ppermute | solution.py:11
Sparse Core Ops, SparseCore 0:
  240.3 298.8 reduce-scatter.1
where the time goes:
time: 549 us; the launch traced here: 548 us
  waiting for transfers between devices  469 us (85%)
  matrix products  22.5 us (4%)
  starting transfers between devices  20.7 us (4%)
  local copies, waits for them, and re-layouts  17 us (3%)
  between operations  14.1 us (3%)
    reduce_scatter x1, waiting for transfers between devices, local(): lax.psum_scatter(jnp.stack(kept, axis=1), 'space', scatter_dimension=2, t...  299 us
    ppermute x8, waiting for transfers between devices, passed_along(): return lax.ppermute(x, axis, [(i, (i + by) % size) for i in range(size)])  170 us
    ppermute x8, starting transfers between devices, passed_along(): return lax.ppermute(x, axis, [(i, (i + by) % size) for i in range(size)])  20.7 us
    dot_general x9, matrix products, tile_product(): lax.dot_general(own, other, (((1,), (1,)), ((), ())), preferred_element_t...  20.6 us
    another operation x1, local copies, waits for them, and re-layouts, local(): jnp.stack(kept, axis=1)  16.7 us
  transfers between devices with their start and end apart: 9, of which 9 were waited for; matrix products, arithmetic and copies ran while one was open for 3% of the time, Pallas kernels for 0%

commit v1 on v0

v1 whole, which is shorter than its diff:
```python
import jax
import jax.numpy as jnp
from jax import lax
from jax.experimental import pallas as pl
from jax.experimental.pallas import tpu as pltpu
from jax.sharding import PartitionSpec as P

ST = 128
MESH = pl.DeviceIdType.MESH
NX, NZ = 4, 8
TILES = 9


def clean_block(snapshots, outlier_cols, outlier_values, threshold):
    block_rows, points = snapshots.shape
    tiles_dev = points // ST
    onehot = (
        outlier_cols[:, :, None] == jnp.arange(tiles_dev, dtype=jnp.int32)[None, None, :]
    ).astype(jnp.bfloat16)
    dense = jnp.einsum("rkos,rkn->rons", outlier_values, onehot, preferred_element_type=jnp.float32)
    dense = dense.reshape(block_rows, points)
    diff = snapshots.astype(jnp.float32) - dense
    return (jnp.sign(diff) * jnp.maximum(jnp.abs(diff) - threshold, 0.0)).astype(jnp.bfloat16)


def kernel(
    clean, out, held, across, passing, part, sent, got, sum_out, sum_in,
    local_sem, g_send, g_recv, r_send, r_recv, f_send, f_recv,
):
    rows = clean.shape[0]
    via_up = passing.shape[0]
    tm, space = lax.axis_index("tm"), lax.axis_index("space")
    core, y, x = tm % 2, (tm // 2) % 2, tm // 4
    z, half = space % NZ, space // NZ

    def device(x=x, y=y, core=core, half=half, z=z):
        return ((x * 2 + y) * 2 + core, half * NZ + z)

    twin = device(core=1 - core)
    beside = device(y=1 - y)
    x_up, x_down = device(x=(x + 1) % NX), device(x=(x + NX - 1) % NX)
    z_up, z_down = device(z=(z + 1) % NZ), device(z=(z + NZ - 1) % NZ)
    far_own, far_beside = device(half=1 - half), device(half=1 - half, y=1 - y)

    load = pltpu.make_async_copy(clean, held.at[core], local_sem)
    load.start()
    barrier = pltpu.get_barrier_semaphore()
    peers = (twin, beside, x_up, x_down, z_up, z_down, far_own, far_beside)
    for peer in peers:
        pl.semaphore_signal(barrier, inc=1, device_id=peer, device_id_type=MESH)
    pl.semaphore_wait(barrier, len(peers))
    load.wait()

    def remote(src, dst, send, recv, to):
        return pltpu.make_async_remote_copy(
            src_ref=src, dst_ref=dst, send_sem=send, recv_sem=recv, device_id=to, device_id_type=MESH
        )

    own = held.at[core]
    mid = via_up // 2
    low, high = pl.ds(0, mid), pl.ds(mid, via_up - mid)
    rest = pl.ds(via_up, rows - via_up)
    copies = [
        (own, held.at[core], twin),
        (own, across, beside),
        (own, held.at[2 + core], x_down),
        (own.at[low], passing.at[low], x_up),
        (own.at[high], passing.at[high], x_up),
        (passing.at[low], held.at[4 + core, low], x_up),
        (passing.at[high], held.at[4 + core, high], x_up),
        (held.at[2 + core, rest], held.at[4 + core, rest], x_down),
        (held.at[2 + core], held.at[2 + core], twin),
        (held.at[4 + core, low], held.at[4 + core, low], twin),
        (held.at[4 + core, high], held.at[4 + core, high], twin),
        (held.at[4 + core, rest], held.at[4 + core, rest], twin),
    ]
    copies = [
        remote(src, dst, g_send.at[n], g_recv.at[n], to) for n, (src, dst, to) in enumerate(copies)
    ]
    for n in range(5):
        copies[n].start()

    def product(place, block, rhs):
        @pl.loop(0, 2)
        def _(q):
            columns = pl.ds(pl.multiple_of(q * 256, 256), 256)
            value = lax.dot_general(
                held[block], rhs[columns, :], (((1,), (1,)), ((), ())), preferred_element_type=jnp.float32
            )
            part[place, :, :, :, columns] = value.reshape(2, NZ, 32, 256)

    ways = ((z_down, -1, 0), (z_up, 1, 1))

    def ring_copy(place, way, step):
        to, _, first = ways[way]
        src, dst = sent.at[place, way, step], got.at[place, way, step]
        if step == 0:
            src, dst = src.at[first], dst.at[first]
        return remote(src, dst, r_send.at[place, way, step], r_recv.at[place, way, step], to)

    def ring_step(place, step):
        for way in range(2):
            _, sign, first = ways[way]
            goal = (z + NZ + sign * (4 - step)) % NZ
            if step > 0:
                ring_copy(place, way, step - 1).wait_recv()
            for h in range(2):
                if step == 0 and h != first:
                    continue
                value = part[place, h, goal]
                if step > 1 or (step == 1 and h == first):
                    value = value + got[place, way, step - 1, h].astype(jnp.float32)
                sent[place, way, step, h] = value.astype(jnp.bfloat16)
            ring_copy(place, way, step).start()

    def is_own(place):
        return place in (0, 1, 2, 7, 8)

    def final_copies(place):
        if is_own(place):
            return [remote(sum_out.at[place, 1 - half], sum_in.at[place, 0], f_send.at[place, 0], f_recv.at[place, 0], far_own)]
        return [
            remote(sum_out.at[place, half], sum_in.at[place, 0], f_send.at[place, 0], f_recv.at[place, 0], beside),
            remote(sum_out.at[place, 1 - half], sum_in.at[place, 1], f_send.at[place, 1], f_recv.at[place, 1], far_beside),
        ]

    def finish(place):
        for way in range(2):
            ring_copy(place, way, 3).wait_recv()
        for h in range(2):
            sum_out[place, h] = (
                part[place, h, z]
                + got[place, 0, 3, h].astype(jnp.float32)
                + got[place, 1, 3, h].astype(jnp.float32)
            )
        for copy in final_copies(place):
            copy.start()

    own_index = (0, 1, 2, None, None, None, None, 3, 4)

    def block_of(place):
        if is_own(place):
            return own_index[place] + core
        if place in (3, 4):
            return 2 + (place - 3)
        return 4 * (1 - y) + (place - 5)

    def distance(place):
        if is_own(place):
            block = block_of(place)
            return 4 * (block // 2) + block % 2 - core
        if place in (3, 4):
            return 2 + 4 * (1 - y) + (place - 3) - core
        return 2 + 4 * y + (place - 5) - core

    def put(place):
        for copy in final_copies(place):
            copy.wait_recv()
        if is_own(place):
            total = sum_out[place, half] + sum_in[place, 0]
        else:
            total = sum_in[place, 0] + sum_in[place, 1]
        out[distance(place)] = total

    def tick(now):
        for step in (3, 2, 1):
            if 0 <= now - step < TILES:
                ring_step(now - step, step)
        if 0 <= now - 4 < TILES:
            finish(now - 4)
        if 0 <= now - 6 < TILES:
            put(now - 6)

    for now in range(TILES + 6):
        if now == 1:
            copies[0].wait_recv()
            for n in (3, 4):
                copies[n].wait_recv()
                copies[n + 2].start()
            copies[2].wait_recv()
            copies[7].start()
            copies[8].start()
            copies[8].wait_recv()
            copies[1].wait_recv()
        if now == 5:
            for n in (5, 6, 7):
                copies[n].wait_recv()
                copies[n + 4 if n < 7 else 11].start()
            for n in (9, 10, 11):
                copies[n].wait_recv()
        if now < TILES:
            product(now, block_of(now), own if is_own(now) else across)
            ring_step(now, 0)
        tick(now)

    for copy in copies:
        copy.wait_send()
    for place in range(TILES):
        for way in range(2):
            for step in range(4):
                ring_copy(place, way, step).wait_send()
        for copy in final_copies(place):
            copy.wait_send()


def local(snapshots, outlier_cols, outlier_values, threshold):
    rows, points = snapshots.shape
    cleaned = clean_block(snapshots, outlier_cols, outlier_values, threshold)
    scale = 1.0 / jnp.sqrt(jnp.float32(points * lax.axis_size("space")))
    via_up = rows * 5 // 8
    piece = rows // (2 * NZ)
    band = pl.pallas_call(
        kernel,
        out_shape=jax.ShapeDtypeStruct((TILES, piece, rows), jnp.float32),
        in_specs=[pl.BlockSpec(memory_space=pl.ANY)],
        out_specs=pl.BlockSpec(memory_space=pltpu.VMEM),
        scratch_shapes=[
            pltpu.VMEM((6, rows, points), jnp.bfloat16),
            pltpu.VMEM((rows, points), jnp.bfloat16),
            pltpu.VMEM((via_up, points), jnp.bfloat16),
            pltpu.VMEM((TILES, 2, NZ, piece, rows), jnp.float32),
            pltpu.VMEM((TILES, 2, 4, 2, piece, rows), jnp.bfloat16),
            pltpu.VMEM((TILES, 2, 4, 2, piece, rows), jnp.bfloat16),
            pltpu.VMEM((TILES, 2, piece, rows), jnp.float32),
            pltpu.VMEM((TILES, 2, piece, rows), jnp.float32),
            pltpu.SemaphoreType.DMA,
            pltpu.SemaphoreType.DMA((12,)),
            pltpu.SemaphoreType.DMA((12,)),
            pltpu.SemaphoreType.DMA((TILES, 2, 4)),
            pltpu.SemaphoreType.DMA((TILES, 2, 4)),
            pltpu.SemaphoreType.DMA((TILES, 2)),
            pltpu.SemaphoreType.DMA((TILES, 2)),
        ],
        compiler_params=pltpu.CompilerParams(
            collective_id=0, has_side_effects=True, vmem_limit_bytes=62 * 1024 * 1024
        ),
    )(cleaned)
    return jnp.transpose(band, (2, 0, 1)) * scale


def solution(mesh):
    placed = (P("tm", "space"), P("tm", "space"), P("tm", "space", None, None), P())
    return jax.shard_map(
        local, mesh=mesh, in_specs=placed, out_specs=P("tm", None, "space"), check_vma=False
    )
```

time: 549 us -> 132 us (0.24)
  waiting for transfers between devices: 469 us -> 0 us
  Pallas kernels: 0 us -> 123 us
  matrix products: 22.5 us -> 1.75 us
  starting transfers between devices: 20.7 us -> 0 us
  local copies, waits for them, and re-layouts: 17 us -> 0.26 us
  between operations: 14.1 us -> 0.83 us
    reduce_scatter x1 -> x0, waiting for transfers between devices: 299 us -> none  [local(): lax.psum_scatter(jnp.stack(kept, axis=1), 'space', scatter_dimension=2, t...]
    ppermute x8 -> x0, waiting for transfers between devices: 170 us -> none  [passed_along(): return lax.ppermute(x, axis, [(i, (i + by) % size) for i in range(size)])]
    pallas_call x0 -> x1, Pallas kernels: none -> 123 us  [local(): pl.pallas_call(kernel, out_shape=jax.ShapeDtypeStruct((TILES, piece, rows...]
    dot_general x10 -> x1, matrix products: 22.5 us -> 1.75 us  [clean_block(): jnp.einsum('rkos,rkn->rons', outlier_values, onehot, preferred_element_ty...]
    ppermute x8 -> x0, starting transfers between devices: 20.7 us -> none  [passed_along(): return lax.ppermute(x, axis, [(i, (i + by) % size) for i in range(size)])]
    another operation x1 -> x0, local copies, waits for them, and re-layouts: 16.7 us -> none  [local(): jnp.stack(kept, axis=1)]
  transfers between devices with their start and end apart: 9 -> 0, of which waited for: 9 -> 0; matrix products, arithmetic and copies ran while one was open for 3% -> 0% of each run, Pallas kernels for 0% -> 0%
where the time goes in v1:
time: 132 us
  Pallas kernels  123 us (93%)
  other arithmetic  5.83 us (4%)
  matrix products  1.75 us (1%)
    pallas_call x1, Pallas kernels, local(): pl.pallas_call(kernel, out_shape=jax.ShapeDtypeStruct((TILES, piece, rows...  123 us
    convert_element_type x1, other arithmetic, clean_block(): (jnp.sign(diff) * jnp.maximum(jnp.abs(diff) - threshold, 0.0)).astype(jnp...  3.89 us

profile of v1, /device:TPU:2, one launch (start us, length us, event | category | flops | bytes accessed | tf_op | source)
XLA Modules:
  0.0 132.1 jit_solution(14734006866931448722)
XLA Ops:
  0.0 0.0 copy-start
  0.0 0.0 copy-start.1
  0.8 0.3 copy-done
  1.1 1.8 %fusion = f32[4,16,128,128]{3,1,2,0:T(8,128)S(1)} fusion(bf16[4,4,128,128]{3,2,1,0:T(8,128)(2,1)S(1)} %copy-done, s32[4,4]{1,0:T(4,128)} %param.5), kind=kOutput, calls=%fused_computation.3 | convolution fusion | flops 8388864 | bytes 4718656 | tf_op jit(solution)/shard_map/rkos,rkn->rons/dot_general | solution.py:20
  2.8 0.0 copy-done.1
  2.8 3.9 %multiply_convert_fusion.clean = bf16[512,2048]{1,0:T(8,128)(2,1)} fusion(f32[64,8,16,128]{3,2,1,0:T(8,128)S(1)} %bitcast.14, bf16[512,2048]{1,0:T(8,128)(2,1)S(1)} %copy-done.1, f32[]{:T(128)S(6)} %copy.13), kind=kLoop, calls=%fused_computation.1 | loop fusion | flops 8388608 | bytes 8388612 | tf_op jit(solution)/shard_map/convert_element_type | solution.py:23
  6.7 123.4 %shard_map.46 = f32[9,32,512]{2,1,0:T(8,128)} custom-call(bf16[512,2048]{1,0:T(8,128)(2,1)} %multiply_convert_fusion.clean), custom_call_target="tpu_custom_call" | custom-call | tf_op jit(solution)/shard_map/pallas_call | solution.py:212
  130.1 1.9 %multiply_bitcast_fusion = f32[512,9,32]{0,2,1:T(8,128)} fusion(f32[9,32,512]{2,1,0:T(8,128)} %shard_map.46), kind=kLoop, calls=%fused_computation.2 | loop fusion | flops 147456 | bytes 1179648 | tf_op jit(solution)/shard_map/mul | solution.py:238
Async XLA Ops:
  0.0 1.1 copy-start
  0.0 2.8 %copy-start.1 = (bf16[512,2048]{1,0:T(8,128)(2,1)S(1)}, bf16[512,2048]{1,0:T(8,128)(2,1)}, u32[]{:S(2)}) copy-start(bf16[512,2048]{1,0:T(8,128)(2,1)} %param.4) | copy-start | bytes 6291460

commit v2 on v0

v2 whole, which is shorter than its diff:
```python
import jax
import jax.numpy as jnp
from jax import lax
from jax.experimental import pallas as pl
from jax.experimental.pallas import tpu as pltpu
from jax.sharding import PartitionSpec as P

MESH = pl.DeviceIdType.MESH
NX, NZ = 4, 8
PARTS = 4
UNITS = 18
DRAINS = (2, 2, 1, 1, 0, 0)


def kernel(
    cols, threshold, snapshots, values, out,
    held, natural, before, part, sent, got, sum_out, sum_in,
    a_send, a_recv, b_send, b_recv, e_send, e_recv, h_send, h_recv,
    tb_send, tb_recv, th_send, th_recv, r_send, r_recv, f_send, f_recv,
):
    rows, points = snapshots.shape
    size = rows // PARTS
    wide = rows // 2
    tm, space = lax.axis_index("tm"), lax.axis_index("space")
    core, y, x = tm % 2, (tm // 2) % 2, tm // 4
    z, half = space % NZ, space // NZ

    def device(x=x, y=y, core=core, half=half, z=z):
        return ((x * 2 + y) * 2 + core, half * NZ + z)

    x_next, x_last = (x + 1) % NX, (x + NX - 1) % NX
    twin = device(core=1 - core)
    beside = device(y=1 - y)
    x_up, x_down = device(x=x_next), device(x=x_last)
    z_up, z_down = device(z=(z + 1) % NZ), device(z=(z + NZ - 1) % NZ)
    far, far_up, far_down = device(half=1 - half), device(x=x_next, half=1 - half), device(x=x_last, half=1 - half)

    barrier = pltpu.get_barrier_semaphore()
    peers = (twin, beside, x_up, x_down, z_up, z_down, far, far_up, far_down)
    for peer in peers:
        pl.semaphore_signal(barrier, inc=1, device_id=peer, device_id_type=MESH)

    tile_rows, tile_points = values.shape[2:]
    limit = threshold[0, 0]

    @pl.loop(0, points // tile_points)
    def _(c):
        lanes = pl.ds(pl.multiple_of(c * tile_points, tile_points), tile_points)
        for r in range(rows // tile_rows):
            across = pl.ds(r * tile_rows, tile_rows)
            dense = jnp.zeros((tile_rows, tile_points), jnp.float32)
            for k in range(values.shape[1]):
                listed = (cols[r, k] == c).astype(jnp.float32)
                dense = dense + listed * values[r, k].astype(jnp.float32)
            diff = snapshots[across, lanes].astype(jnp.float32) - dense
            shrunk = diff - jnp.clip(diff, -limit, limit)
            natural[across, lanes] = shrunk.astype(jnp.bfloat16)
            groups = shrunk.reshape(tile_rows // 32, PARTS, 8, tile_points)
            for n in range(PARTS):
                piece = groups[:, n].reshape(tile_rows // PARTS, tile_points)
                held[core, pl.ds(n * size + r * (tile_rows // PARTS), tile_rows // PARTS), lanes] = piece.astype(jnp.bfloat16)

    pl.semaphore_wait(barrier, len(peers))

    def remote(src, dst, send, recv, to):
        return pltpu.make_async_remote_copy(
            src_ref=src, dst_ref=dst, send_sem=send, recv_sem=recv, device_id=to, device_id_type=MESH
        )

    def portion(block, n):
        return held.at[block, pl.ds(n * size, size)]

    a_copy = [remote(portion(core, n), portion(core, n), a_send.at[n], a_recv.at[n], twin) for n in range(PARTS)]
    b_copy = [remote(portion(core, n), portion(2 + core, n), b_send.at[n], b_recv.at[n], x_down) for n in range(PARTS)]
    e_copy = [
        remote(natural.at[pl.ds(q * wide, wide)], before.at[pl.ds(q * wide, wide)], e_send.at[q], e_recv.at[q], x_up)
        for q in range(2)
    ]
    h_from = core + 2 * (1 - y)
    h_copy = [remote(portion(h_from, n), portion(4 + core, n), h_send.at[n], h_recv.at[n], beside) for n in range(PARTS)]
    tb_copy = [remote(portion(2 + core, n), portion(2 + core, n), tb_send.at[n], tb_recv.at[n], twin) for n in range(PARTS)]
    th_copy = [remote(portion(4 + core, n), portion(4 + core, n), th_send.at[n], th_recv.at[n], twin) for n in range(PARTS)]
    gathers = a_copy + b_copy + e_copy + h_copy + tb_copy + th_copy
    for copy in a_copy[:1] + b_copy[:1] + e_copy[:1] + a_copy[1:] + b_copy[1:] + e_copy[1:]:
        copy.start()

    def aa(n):
        return ("a", 0, (core, 1), (n * (1 + core), n * (1 + core) + core))

    def ab(n):
        return ("a", 4, (2, 3), (n, n))

    def ah(n):
        return ("a", 2, (4, 5), (n, n))

    def eh(q, n):
        return ("e", 6, (4, 5), (n, n), q)

    def eb(q, n):
        return ("e", 8, (2, 3), (n, n), q)

    def eb_last(q):
        return ("e", 8, (2, 2 + core), (core, 1), q)

    rounds = (
        ((aa(0),), (aa(1),)),
        ((ab(0),),),
        ((ab(1),), (ah(0),), (aa(2), eb(0, 0))),
        ((ab(2),), (ah(1),), (eh(0, 0),)),
        ((ab(3),), (ah(2),), (aa(3), eb(1, 0)), (eb_last(0),), (eb_last(1),), (eh(1, 0),)),
        ((ah(3),), (eh(0, 1),), (eh(1, 1),)),
    )
    units = [unit for group in rounds for unit in group]

    def each(place, action):
        if len(units[place]) == 1:
            action(units[place][0])
        else:
            for n, unit in enumerate(units[place]):
                @pl.when(core == n)
                def _(unit=unit):
                    action(unit)

    def rows_of(block, n, count):
        return held[block, pl.ds(pl.multiple_of(n * count, count), count), :]

    def times(left, right):
        return lax.dot_general(left, right, (((1,), (1,)), ((), ())), preferred_element_type=jnp.float32)

    def product(place):
        def action(unit):
            kind, _, blocks, parts = unit[:4]
            if kind == "a":
                left = jnp.concatenate([rows_of(b, n, size) for b, n in zip(blocks, parts)], axis=0)

                @pl.loop(0, 2)
                def _(q):
                    columns = pl.ds(pl.multiple_of(q * wide, wide), wide)
                    value = times(left, natural[columns, :]).reshape(2, 2, NZ, 8, wide)
                    for i in range(2):
                        part[place, :, :, pl.ds(8 * i, 8), columns] = value[i]
            else:
                q = unit[4]
                right = before[pl.ds(q * wide, wide), :]
                for i, (b, n) in enumerate(zip(blocks, parts)):
                    value = times(rows_of(b, n, 2 * size), right).reshape(2, 2, NZ, 8, wide)
                    for j in range(2):
                        part[place, :, :, pl.ds(8 * j, 8), pl.ds(i * wide, wide)] = value[j]

        each(place, action)

    ways = ((z_down, -1, 0), (z_up, 1, 1))

    def ring_copy(place, way, step):
        to, _, first = ways[way]
        src, dst = sent.at[place, way, step], got.at[place, way, step]
        if step == 0:
            src, dst = src.at[first], dst.at[first]
        return remote(src, dst, r_send.at[place, way, step], r_recv.at[place, way, step], to)

    def ring_step(place, step):
        for way in range(2):
            _, sign, first = ways[way]
            goal = (z + NZ + sign * (4 - step)) % NZ
            if step > 0:
                ring_copy(place, way, step - 1).wait_recv()
            for h in range(2):
                if step == 0 and h != first:
                    continue
                value = part[place, h, goal]
                if step > 1 or (step == 1 and h == first):
                    value = value + got[place, way, step - 1, h].astype(jnp.float32)
                sent[place, way, step, h] = value.astype(jnp.bfloat16)
            ring_copy(place, way, step).start()

    def final_copies(place, unit):
        def copy(h, n, to):
            return remote(sum_out.at[place, h], sum_in.at[place, n], f_send.at[place, n], f_recv.at[place, n], to)

        if unit[0] == "a":
            return [copy(1 - half, 0, far)]
        return [copy(half, 0, x_down), copy(1 - half, 1, far_down)]

    def finish(place):
        for way in range(2):
            ring_copy(place, way, 3).wait_recv()
        for h in range(2):
            sum_out[place, h] = (
                part[place, h, z]
                + got[place, 0, 3, h].astype(jnp.float32)
                + got[place, 1, 3, h].astype(jnp.float32)
            )

        def action(unit):
            for copy in final_copies(place, unit):
                copy.start()

        each(place, action)

    def put(place):
        def action(unit):
            kind, base, blocks, parts = unit[:4]
            for copy in final_copies(place, unit):
                copy.wait_recv()
            if kind == "a":
                total = sum_out[place, half] + sum_in[place, 0]
            else:
                total = sum_in[place, 0] + sum_in[place, 1]
            for i, (b, n) in enumerate(zip(blocks, parts)):
                k = base + b % 2 - core
                if kind == "a":
                    out[k, pl.ds(pl.multiple_of(8 * n, 8), 8), :] = total[8 * i : 8 * i + 8]
                else:
                    q = unit[4]
                    out[k, pl.ds(pl.multiple_of(16 * n, 16), 16), pl.ds(q * wide, wide)] = total[:, i * wide : (i + 1) * wide]

        each(place, action)

    flying = []

    def advance():
        for entry in list(flying):
            place, stage = entry
            if stage < 4:
                ring_step(place, stage)
            elif stage == 4:
                finish(place)
            elif stage == 6:
                put(place)
                flying.remove(entry)
                continue
            entry[1] += 1

    def arrive(number):
        if number == 0:
            a_copy[0].wait_recv()
            a_copy[1].wait_recv()
            return
        if number <= PARTS:
            b_copy[number - 1].wait_recv()
            h_copy[number - 1].start()
            tb_copy[number - 1].start()
        if number >= 2:
            h_copy[number - 2].wait_recv()
            th_copy[number - 2].start()
        if number == 2:
            a_copy[2].wait_recv()
            a_copy[3].wait_recv()
            e_copy[0].wait_recv()
        if number == 4:
            e_copy[1].wait_recv()
        if number <= PARTS:
            tb_copy[number - 1].wait_recv()
        if number >= 2:
            th_copy[number - 2].wait_recv()

    place = 0
    for number, group in enumerate(rounds):
        arrive(number)
        for _ in group:
            advance()
            product(place)
            ring_step(place, 0)
            flying.append([place, 1])
            place += 1
        for _ in range(DRAINS[number]):
            advance()
    while flying:
        advance()

    for copy in gathers:
        copy.wait_send()
    for place in range(UNITS):
        for way in range(2):
            for step in range(4):
                ring_copy(place, way, step).wait_send()

        def sent_all(unit, place=place):
            for copy in final_copies(place, unit):
                copy.wait_send()

        each(place, sent_all)


def local(snapshots, outlier_cols, outlier_values, threshold):
    rows, points = snapshots.shape
    scale = 1.0 / jnp.sqrt(jnp.float32(points * lax.axis_size("space")))
    dma = pltpu.SemaphoreType.DMA
    pairs = [PARTS, PARTS, 2, PARTS, PARTS, PARTS]
    band = pl.pallas_call(
        kernel,
        out_shape=jax.ShapeDtypeStruct((9, 32, rows), jnp.float32),
        in_specs=[pl.BlockSpec(memory_space=pltpu.SMEM)] * 2 + [pl.BlockSpec(memory_space=pltpu.VMEM)] * 2,
        out_specs=pl.BlockSpec(memory_space=pltpu.VMEM),
        scratch_shapes=[
            pltpu.VMEM((6, rows, points), jnp.bfloat16),
            pltpu.VMEM((rows, points), jnp.bfloat16),
            pltpu.VMEM((rows, points), jnp.bfloat16),
            pltpu.VMEM((UNITS, 2, NZ, 16, rows), jnp.float32),
            pltpu.VMEM((UNITS, 2, 4, 2, 16, rows), jnp.bfloat16),
            pltpu.VMEM((UNITS, 2, 4, 2, 16, rows), jnp.bfloat16),
            pltpu.VMEM((UNITS, 2, 16, rows), jnp.float32),
            pltpu.VMEM((UNITS, 2, 16, rows), jnp.float32),
            *[dma((n,)) for count in pairs for n in (count, count)],
            dma((UNITS, 2, 4)),
            dma((UNITS, 2, 4)),
            dma((UNITS, 2)),
            dma((UNITS, 2)),
        ],
        compiler_params=pltpu.CompilerParams(
            collective_id=0, has_side_effects=True, vmem_limit_bytes=58 * 1024 * 1024
        ),
    )(outlier_cols, threshold.reshape(1, 1), snapshots, outlier_values)
    return jnp.transpose(band, (2, 0, 1)) * scale


def solution(mesh):
    placed = (P("tm", "space"), P("tm", "space"), P("tm", "space", None, None), P())
    return jax.shard_map(
        local, mesh=mesh, in_specs=placed, out_specs=P("tm", None, "space"), check_vma=False
    )
```

time: 549 us -> 136 us (0.25)
  waiting for transfers between devices: 469 us -> 0 us
  Pallas kernels: 0 us -> 133 us
  matrix products: 22.5 us -> 0 us
  starting transfers between devices: 20.7 us -> 0 us
  local copies, waits for them, and re-layouts: 17 us -> 0 us
  between operations: 14.1 us -> 0.66 us
    reduce_scatter x1 -> x0, waiting for transfers between devices: 299 us -> none  [local(): lax.psum_scatter(jnp.stack(kept, axis=1), 'space', scatter_dimension=2, t...]
    ppermute x8 -> x0, waiting for transfers between devices: 170 us -> none  [passed_along(): return lax.ppermute(x, axis, [(i, (i + by) % size) for i in range(size)])]
    pallas_call x0 -> x1, Pallas kernels: none -> 133 us  [local(): pl.pallas_call(kernel, out_shape=jax.ShapeDtypeStruct((9, 32, rows), jnp....]
    dot_general x10 -> x0, matrix products: 22.5 us -> none  [the longest x9 20.6 us: tile_product(): lax.dot_general(own, other, (((1,), (1,)), ((), ())), preferred_element_t...]
    ppermute x8 -> x0, starting transfers between devices: 20.7 us -> none  [passed_along(): return lax.ppermute(x, axis, [(i, (i + by) % size) for i in range(size)])]
    another operation x1 -> x0, local copies, waits for them, and re-layouts: 16.7 us -> none  [local(): jnp.stack(kept, axis=1)]
  transfers between devices with their start and end apart: 9 -> 0, of which waited for: 9 -> 0; matrix products, arithmetic and copies ran while one was open for 3% -> 0% of each run, Pallas kernels for 0% -> 0%
where the time goes in v2:
time: 136 us; the launch traced here: 135 us
  Pallas kernels  133 us (98%)
  other arithmetic  1.94 us (1%)
    pallas_call x1, Pallas kernels, local(): pl.pallas_call(kernel, out_shape=jax.ShapeDtypeStruct((9, 32, rows), jnp....  133 us

profile of v2, /device:TPU:2, one launch (start us, length us, event | category | flops | bytes accessed | tf_op | source)
XLA Modules:
  0.0 135.5 jit_solution(6514155246406750255)
XLA Ops:
  0.7 132.9 %shard_map.46 = f32[9,32,512]{2,1,0:T(8,128)} custom-call(s32[4,4]{1,0:T(4,128)} %cols.1, f32[1,1]{1,0:T(1,128)} %bitcast.3.threshold, bf16[512,2048]{1,0:T(8,128)(2,1)} %snapshots.1, bf16[4,4,128,128]{3,2,1,0:T(8,128)(2,1)} %values.1), custom_call_target="tpu_custom_call" | custom-call | tf_op jit(solution)/shard_map/pallas_call | solution.py:290
  133.5 1.9 %multiply_bitcast_fusion = f32[512,9,32]{0,2,1:T(8,128)} fusion(f32[9,32,512]{2,1,0:T(8,128)} %shard_map.46), kind=kLoop, calls=%fused_computation | loop fusion | flops 147456 | bytes 1179648 | tf_op jit(solution)/shard_map/mul | solution.py:314

commit v3 on v2

--- a/solution.py
+++ b/solution.py
@@ -7,16 +7,96 @@
 
 MESH = pl.DeviceIdType.MESH
 NX, NZ = 4, 8
-PARTS = 4
+PARTS, PIECES = 4, 8
 UNITS = 18
-DRAINS = (2, 2, 1, 1, 0, 0)
+
+NEEDS = (
+    (("a", 1),), (("a", 2),),
+    (("b", 1),),
+    (("b", 2),), (("h", 1),), (("a", 3), ("b", 2), ("e", 1)),
+    (("b", 3),), (("h", 2),), (("h", 2), ("e", 1)),
+    (("b", 4),), (("h", 3),), (("a", 4), ("b", 2), ("e", 2)),
+    (("b", 4), ("e", 1)), (("b", 4), ("e", 2)), (("h", 2), ("e", 2)),
+    (("h", 4), ("e", 1)), (("h", 4), ("e", 2)), (("h", 4),),
+)
+
+
+def plan():
+    rate, twin_rate, hop, twin_hop, multiply, add = 45.0, 220.0, 2.0, 1.0, 0.85, 0.12
+    free, there, now, order = {}, {}, 0.0, []
+
+    def send(link, size, latency=hop, speed=rate):
+        free[link] = max(now, free.get(link, 0.0)) + size / speed
+        return free[link] + latency
+
+    piece = 2048 / PIECES
+    for n in range(PIECES):
+        there["a", n] = send("twin", piece, twin_hop, twin_rate)
+        there["b", n] = send("down", piece)
+    for n in range(2):
+        there["e", n] = send("up", 1024)
+    waiting = [(kind, n) for kind in "bh" for n in range(PIECES)]
+    todo, flying = list(range(UNITS)), {}
+    passed = {"a": "a", "b": "tb", "h": "th"}
+    while todo or flying:
+        choice = []
+        for kind in "bh":
+            left = [n for k, n in waiting if k == kind]
+            if left and (kind, left[0]) in there:
+                choice.append((there[kind, left[0]], 0, left[0], 0, (kind, left[0])))
+        for unit in todo:
+            keys = [
+                (passed.get(k, k), n)
+                for k, count in NEEDS[unit]
+                for n in range(count * (1 if k == "e" else PIECES // PARTS))
+            ]
+            if all(key in there for key in keys):
+                choice.append((max(there[key] for key in keys), 2, unit, 0, ("unit", unit)))
+        for unit, at in flying.items():
+            for way in range(2):
+                step = at[way]
+                if step < 4:
+                    choice.append((at[way, step - 1], 1, unit, step, ("hop", unit, way, step)))
+            if "sum" in at:
+                choice.append((at["sum"], 3, unit, 5, ("put", unit)))
+            elif at[0] == at[1] == 4:
+                choice.append((max(at[0, 3], at[1, 3]), 1, unit, 4, ("sum", unit)))
+        now = max(now, min(c[0] for c in choice))
+        action = min((c for c in choice if c[0] <= now), key=lambda c: c[1:4])[4]
+        order.append(action)
+        kind, n = action[:2]
+        if kind == "b":
+            waiting.remove(action)
+            there["h", n] = send("beside", piece)
+            there["tb", n] = send("twin", piece, twin_hop, twin_rate)
+        elif kind == "h":
+            waiting.remove(action)
+            there["th", n] = send("twin", piece, twin_hop, twin_rate)
+        elif kind == "unit":
+            todo.remove(n)
+            now += multiply + add
+            flying[n] = {way: 1 for way in range(2)}
+            for way in range(2):
+                flying[n][way, 0] = send(way, 16)
+        elif kind == "hop":
+            way, step = action[2:]
+            now += add
+            flying[n][way, step] = send(way, 32)
+            flying[n][way] = step + 1
+        elif kind == "sum":
+            now += add
+            flying[n]["sum"] = send("far", 40, hop + 1.5)
+        else:
+            now += add
+            del flying[n]
+    return order
 
 
 def kernel(
-    cols, threshold, snapshots, values, out,
-    held, natural, before, part, sent, got, sum_out, sum_in,
-    a_send, a_recv, b_send, b_recv, e_send, e_recv, h_send, h_recv,
-    tb_send, tb_recv, th_send, th_recv, r_send, r_recv, f_send, f_recv,
+    cols, threshold, snapshots_in, values_in, out,
+    snapshots, values, held, natural, before, part, sent, got, sum_out, sum_in,
+    in_sem, g_send, a_recv, b_recv, e_recv, h_recv, tb_recv, th_recv,
+    first_send, r_send, r_recv, f_send, f_recv,
 ):
     rows, points = snapshots.shape
     size = rows // PARTS
@@ -39,6 +119,14 @@
     peers = (twin, beside, x_up, x_down, z_up, z_down, far, far_up, far_down)
     for peer in peers:
         pl.semaphore_signal(barrier, inc=1, device_id=peer, device_id_type=MESH)
+    loads = [
+        pltpu.make_async_copy(values_in, values, in_sem.at[0]),
+        pltpu.make_async_copy(snapshots_in, snapshots, in_sem.at[1]),
+    ]
+    for load in loads:
+        load.start()
+    for load in loads:
+        load.wait()
 
     tile_rows, tile_points = values.shape[2:]
     limit = threshold[0, 0]
@@ -68,19 +156,18 @@
         )
 
     def portion(block, n):
-        return held.at[block, pl.ds(n * size, size)]
-
-    a_copy = [remote(portion(core, n), portion(core, n), a_send.at[n], a_recv.at[n], twin) for n in range(PARTS)]
-    b_copy = [remote(portion(core, n), portion(2 + core, n), b_send.at[n], b_recv.at[n], x_down) for n in range(PARTS)]
+        return held.at[block, pl.ds(n * (rows // PIECES), rows // PIECES)]
+
+    a_copy = [remote(portion(core, n), portion(core, n), g_send, a_recv.at[n], twin) for n in range(PIECES)]
+    b_copy = [remote(portion(core, n), portion(2 + core, n), g_send, b_recv.at[n], x_down) for n in range(PIECES)]
     e_copy = [
-        remote(natural.at[pl.ds(q * wide, wide)], before.at[pl.ds(q * wide, wide)], e_send.at[q], e_recv.at[q], x_up)
+        remote(natural.at[pl.ds(q * wide, wide)], before.at[pl.ds(q * wide, wide)], g_send, e_recv.at[q], x_up)
         for q in range(2)
     ]
     h_from = core + 2 * (1 - y)
-    h_copy = [remote(portion(h_from, n), portion(4 + core, n), h_send.at[n], h_recv.at[n], beside) for n in range(PARTS)]
-    tb_copy = [remote(portion(2 + core, n), portion(2 + core, n), tb_send.at[n], tb_recv.at[n], twin) for n in range(PARTS)]
-    th_copy = [remote(portion(4 + core, n), portion(4 + core, n), th_send.at[n], th_recv.at[n], twin) for n in range(PARTS)]
-    gathers = a_copy + b_copy + e_copy + h_copy + tb_copy + th_copy
+    h_copy = [remote(portion(h_from, n), portion(4 + core, n), g_send, h_recv.at[n], beside) for n in range(PIECES)]
+    tb_copy = [remote(portion(2 + core, n), portion(2 + core, n), g_send, tb_recv.at[n], twin) for n in range(PIECES)]
+    th_copy = [remote(portion(4 + core, n), portion(4 + core, n), g_send, th_recv.at[n], twin) for n in range(PIECES)]
     for copy in a_copy[:1] + b_copy[:1] + e_copy[:1] + a_copy[1:] + b_copy[1:] + e_copy[1:]:
         copy.start()
 
@@ -108,7 +195,7 @@
         ((ab(1),), (ah(0),), (aa(2), eb(0, 0))),
         ((ab(2),), (ah(1),), (eh(0, 0),)),
         ((ab(3),), (ah(2),), (aa(3), eb(1, 0)), (eb_last(0),), (eb_last(1),), (eh(1, 0),)),
-        ((ah(3),), (eh(0, 1),), (eh(1, 1),)),
+        ((eh(0, 1),), (eh(1, 1),), (ah(3),)),
     )
     units = [unit for group in rounds for unit in group]
 
@@ -156,22 +243,21 @@
         src, dst = sent.at[place, way, step], got.at[place, way, step]
         if step == 0:
             src, dst = src.at[first], dst.at[first]
-        return remote(src, dst, r_send.at[place, way, step], r_recv.at[place, way, step], to)
-
-    def ring_step(place, step):
-        for way in range(2):
-            _, sign, first = ways[way]
-            goal = (z + NZ + sign * (4 - step)) % NZ
-            if step > 0:
-                ring_copy(place, way, step - 1).wait_recv()
-            for h in range(2):
-                if step == 0 and h != first:
-                    continue
-                value = part[place, h, goal]
-                if step > 1 or (step == 1 and h == first):
-                    value = value + got[place, way, step - 1, h].astype(jnp.float32)
-                sent[place, way, step, h] = value.astype(jnp.bfloat16)
-            ring_copy(place, way, step).start()
+        return remote(src, dst, r_send if step else first_send, r_recv.at[place, way, step], to)
+
+    def hop(place, way, step):
+        _, sign, first = ways[way]
+        goal = (z + NZ + sign * (4 - step)) % NZ
+        if step > 0:
+            ring_copy(place, way, step - 1).wait_recv()
+        for h in range(2):
+            if step == 0 and h != first:
+                continue
+            value = part[place, h, goal]
+            if step > 1 or (step == 1 and h == first):
+                value = value + got[place, way, step - 1, h].astype(jnp.float32)
+            sent[place, way, step, h] = value.astype(jnp.bfloat16)
+        ring_copy(place, way, step).start()
 
     def final_copies(place, unit):
         def copy(h, n, to):
@@ -216,65 +302,42 @@
 
         each(place, action)
 
-    flying = []
-
-    def advance():
-        for entry in list(flying):
-            place, stage = entry
-            if stage < 4:
-                ring_step(place, stage)
-            elif stage == 4:
-                finish(place)
-            elif stage == 6:
-                put(place)
-                flying.remove(entry)
-                continue
-            entry[1] += 1
-
-    def arrive(number):
-        if number == 0:
-            a_copy[0].wait_recv()
-            a_copy[1].wait_recv()
-            return
-        if number <= PARTS:
-            b_copy[number - 1].wait_recv()
-            h_copy[number - 1].start()
-            tb_copy[number - 1].start()
-        if number >= 2:
-            h_copy[number - 2].wait_recv()
-            th_copy[number - 2].start()
-        if number == 2:
-            a_copy[2].wait_recv()
-            a_copy[3].wait_recv()
-            e_copy[0].wait_recv()
-        if number == 4:
-            e_copy[1].wait_recv()
-        if number <= PARTS:
-            tb_copy[number - 1].wait_recv()
-        if number >= 2:
-            th_copy[number - 2].wait_recv()
-
-    place = 0
-    for number, group in enumerate(rounds):
-        arrive(number)
-        for _ in group:
-            advance()
-            product(place)
-            ring_step(place, 0)
-            flying.append([place, 1])
-            place += 1
-        for _ in range(DRAINS[number]):
-            advance()
-    while flying:
-        advance()
-
-    for copy in gathers:
-        copy.wait_send()
+    copies = {"a": a_copy, "b": tb_copy, "h": th_copy, "e": e_copy}
+    waited = {kind: 0 for kind in copies}
+
+    def need(kind, count):
+        count *= 1 if kind == "e" else PIECES // PARTS
+        for n in range(waited[kind], count):
+            copies[kind][n].wait_recv()
+        waited[kind] = max(waited[kind], count)
+
+    for kind, n, *rest in plan():
+        if kind == "b":
+            b_copy[n].wait_recv()
+            h_copy[n].start()
+            tb_copy[n].start()
+        elif kind == "h":
+            h_copy[n].wait_recv()
+            th_copy[n].start()
+        elif kind == "unit":
+            for what, count in NEEDS[n]:
+                need(what, count)
+            product(n)
+            for way in range(2):
+                hop(n, way, 0)
+        elif kind == "hop":
+            hop(n, *rest)
+        elif kind == "sum":
+            finish(n)
+        else:
+            put(n)
+
+    remote(held, held, g_send, a_recv.at[0], twin).wait_send()
+    steps = sent.at[:, :, pl.ds(1, 3)]
+    remote(steps, steps, r_send, a_recv.at[0], twin).wait_send()
+    firsts = sent.at[:, :, 0, 0]
+    remote(firsts, firsts, first_send, a_recv.at[0], twin).wait_send()
     for place in range(UNITS):
-        for way in range(2):
-            for step in range(4):
-                ring_copy(place, way, step).wait_send()
-
         def sent_all(unit, place=place):
             for copy in final_copies(place, unit):
                 copy.wait_send()
@@ -286,13 +349,14 @@
     rows, points = snapshots.shape
     scale = 1.0 / jnp.sqrt(jnp.float32(points * lax.axis_size("space")))
     dma = pltpu.SemaphoreType.DMA
-    pairs = [PARTS, PARTS, 2, PARTS, PARTS, PARTS]
     band = pl.pallas_call(
         kernel,
         out_shape=jax.ShapeDtypeStruct((9, 32, rows), jnp.float32),
-        in_specs=[pl.BlockSpec(memory_space=pltpu.SMEM)] * 2 + [pl.BlockSpec(memory_space=pltpu.VMEM)] * 2,
+        in_specs=[pl.BlockSpec(memory_space=pltpu.SMEM)] * 2 + [pl.BlockSpec(memory_space=pl.ANY)] * 2,
         out_specs=pl.BlockSpec(memory_space=pltpu.VMEM),
         scratch_shapes=[
+            pltpu.VMEM(snapshots.shape, jnp.bfloat16),
+            pltpu.VMEM(outlier_values.shape, jnp.bfloat16),
             pltpu.VMEM((6, rows, points), jnp.bfloat16),
             pltpu.VMEM((rows, points), jnp.bfloat16),
             pltpu.VMEM((rows, points), jnp.bfloat16),
@@ -301,8 +365,11 @@
             pltpu.VMEM((UNITS, 2, 4, 2, 16, rows), jnp.bfloat16),
             pltpu.VMEM((UNITS, 2, 16, rows), jnp.float32),
             pltpu.VMEM((UNITS, 2, 16, rows), jnp.float32),
-            *[dma((n,)) for count in pairs for n in (count, count)],
-            dma((UNITS, 2, 4)),
+            dma((2,)),
+            dma,
+            *[dma((count,)) for count in (PIECES, PIECES, 2, PIECES, PIECES, PIECES)],
+            dma,
+            dma,
             dma((UNITS, 2, 4)),
             dma((UNITS, 2)),
             dma((UNITS, 2)),

time: 136 us -> 104 us (0.76)
  Pallas kernels: 133 us -> 101 us
    pallas_call x1, Pallas kernels: 133 us -> 101 us  [local(): pl.pallas_call(kernel, out_shape=jax.ShapeDtypeStruct((9, 32, rows), jnp....]
where the time goes in v3:
time: 104 us; the launch traced here: 103 us
  Pallas kernels  101 us (97%)
  other arithmetic  1.94 us (2%)
    pallas_call x1, Pallas kernels, local(): pl.pallas_call(kernel, out_shape=jax.ShapeDtypeStruct((9, 32, rows), jnp....  101 us

profile of v3, /device:TPU:2, one launch (start us, length us, event | category | flops | bytes accessed | tf_op | source)
XLA Modules:
  0.0 103.4 jit_solution(12236072899483616951)
XLA Ops:
  0.7 100.8 %shard_map.46 = f32[9,32,512]{2,1,0:T(8,128)} custom-call(s32[4,4]{1,0:T(4,128)} %cols.1, f32[1,1]{1,0:T(1,128)} %bitcast.3.threshold, bf16[512,2048]{1,0:T(8,128)(2,1)} %snapshots_in.1, bf16[4,4,128,128]{3,2,1,0:T(8,128)(2,1)} %values_in.1), custom_call_target="tpu_custom_call" | custom-call | tf_op jit(solution)/shard_map/pallas_call | solution.py:352
  101.4 1.9 %multiply_bitcast_fusion = f32[512,9,32]{0,2,1:T(8,128)} fusion(f32[9,32,512]{2,1,0:T(8,128)} %shard_map.46), kind=kLoop, calls=%fused_computation | loop fusion | flops 147456 | bytes 1179648 | tf_op jit(solution)/shard_map/mul | solution.py:381

commit v4 on v3

--- a/solution.py
+++ b/solution.py
@@ -7,7 +7,7 @@
 
 MESH = pl.DeviceIdType.MESH
 NX, NZ = 4, 8
-PARTS, PIECES = 4, 8
+PARTS, PIECES = 4, 16
 UNITS = 18
 
 NEEDS = (
@@ -22,7 +22,7 @@
 
 
 def plan():
-    rate, twin_rate, hop, twin_hop, multiply, add = 45.0, 220.0, 2.0, 1.0, 0.85, 0.12
+    rate, twin_rate, hop, twin_hop, multiply, add = 44.0, 220.0, 3.5, 2.0, 0.85, 0.15
     free, there, now, order = {}, {}, 0.0, []
 
     def send(link, size, latency=hop, speed=rate):
@@ -261,7 +261,7 @@
 
     def final_copies(place, unit):
         def copy(h, n, to):
-            return remote(sum_out.at[place, h], sum_in.at[place, n], f_send.at[place, n], f_recv.at[place, n], to)
+            return remote(sum_out.at[place, h], sum_in.at[place, n], f_send, f_recv.at[place, n], to)
 
         if unit[0] == "a":
             return [copy(1 - half, 0, far)]
@@ -337,12 +337,13 @@
     remote(steps, steps, r_send, a_recv.at[0], twin).wait_send()
     firsts = sent.at[:, :, 0, 0]
     remote(firsts, firsts, first_send, a_recv.at[0], twin).wait_send()
-    for place in range(UNITS):
-        def sent_all(unit, place=place):
-            for copy in final_copies(place, unit):
-                copy.wait_send()
-
-        each(place, sent_all)
+    for n in range(2):
+        count = sum(1 if unit[min(n, len(unit) - 1)][0] == "a" else 2 for unit in units)
+
+        @pl.when(core == n)
+        def _(count=count):
+            sums = sum_out.at[pl.ds(0, count // 2)]
+            remote(sums, sums, f_send, a_recv.at[0], twin).wait_send()
 
 
 def local(snapshots, outlier_cols, outlier_values, threshold):
@@ -371,7 +372,7 @@
             dma,
             dma,
             dma((UNITS, 2, 4)),
-            dma((UNITS, 2)),
+            dma,
             dma((UNITS, 2)),
         ],
         compiler_params=pltpu.CompilerParams(

time: 104 us -> 99.2 us (0.954)
  Pallas kernels: 101 us -> 96.4 us
    pallas_call x1, Pallas kernels: 101 us -> 96.4 us  [local(): pl.pallas_call(kernel, out_shape=jax.ShapeDtypeStruct((9, 32, rows), jnp....]
where the time goes in v4:
time: 99.2 us; the launch traced here: 99 us
  Pallas kernels  96.4 us (97%)
  other arithmetic  1.94 us (2%)
    pallas_call x1, Pallas kernels, local(): pl.pallas_call(kernel, out_shape=jax.ShapeDtypeStruct((9, 32, rows), jnp....  96.4 us

profile of v4, /device:TPU:2, one launch (start us, length us, event | category | flops | bytes accessed | tf_op | source)
XLA Modules:
  0.0 99.0 jit_solution(10047660933138217639)
XLA Ops:
  0.7 96.4 %shard_map.46 = f32[9,32,512]{2,1,0:T(8,128)} custom-call(s32[4,4]{1,0:T(4,128)} %cols.1, f32[1,1]{1,0:T(1,128)} %bitcast.3.threshold, bf16[512,2048]{1,0:T(8,128)(2,1)} %snapshots_in.1, bf16[4,4,128,128]{3,2,1,0:T(8,128)(2,1)} %values_in.1), custom_call_target="tpu_custom_call" | custom-call | tf_op jit(solution)/shard_map/pallas_call | solution.py:353
  97.1 1.9 %multiply_bitcast_fusion = f32[512,9,32]{0,2,1:T(8,128)} fusion(f32[9,32,512]{2,1,0:T(8,128)} %shard_map.46), kind=kLoop, calls=%fused_computation | loop fusion | flops 147456 | bytes 1179648 | tf_op jit(solution)/shard_map/mul | solution.py:382

commit v5 on v4

--- a/solution.py
+++ b/solution.py
@@ -10,18 +10,19 @@
 PARTS, PIECES = 4, 16
 UNITS = 18
 
+
+BOTH = {
+    2: (("b", 1),), 3: (("b", 2),), 4: (("h", 1),), 6: (("b", 3),), 7: (("h", 2),), 8: (("h", 2), ("e", 1)),
+    9: (("b", 4),), 10: (("h", 3),), 13: (("b", 4), ("e", 2)), 14: (("h", 2), ("e", 2)),
+    15: (("b", 4), ("h", 4), ("e", 1)), 16: (("h", 4), ("e", 2)), 17: (("h", 4),),
+}
 NEEDS = (
-    (("a", 1),), (("a", 2),),
-    (("b", 1),),
-    (("b", 2),), (("h", 1),), (("a", 3), ("b", 2), ("e", 1)),
-    (("b", 3),), (("h", 2),), (("h", 2), ("e", 1)),
-    (("b", 4),), (("h", 3),), (("a", 4), ("b", 2), ("e", 2)),
-    (("b", 4), ("e", 1)), (("b", 4), ("e", 2)), (("h", 2), ("e", 2)),
-    (("h", 4), ("e", 1)), (("h", 4), ("e", 2)), (("h", 4),),
+    BOTH | {12: (("b", 2), ("h", 3), ("e", 1)), 0: (("a", 1),), 1: (("a", 2),), 5: (("a", 3),), 11: (("a", 4),)},
+    BOTH | {12: (("b", 3), ("h", 3), ("e", 1)), 0: (), 1: (), 5: (("b", 2), ("e", 1)), 11: (("b", 2), ("e", 2))},
 )
 
 
-def plan():
+def plan(needs):
     rate, twin_rate, hop, twin_hop, multiply, add = 44.0, 220.0, 3.5, 2.0, 0.85, 0.15
     free, there, now, order = {}, {}, 0.0, []
 
@@ -47,11 +48,11 @@
         for unit in todo:
             keys = [
                 (passed.get(k, k), n)
-                for k, count in NEEDS[unit]
+                for k, count in needs[unit]
                 for n in range(count * (1 if k == "e" else PIECES // PARTS))
             ]
             if all(key in there for key in keys):
-                choice.append((max(there[key] for key in keys), 2, unit, 0, ("unit", unit)))
+                choice.append((max((there[key] for key in keys), default=now), 2, unit, 0, ("unit", unit)))
         for unit, at in flying.items():
             for way in range(2):
                 step = at[way]
@@ -181,32 +182,34 @@
         return ("a", 2, (4, 5), (n, n))
 
     def eh(q, n):
-        return ("e", 6, (4, 5), (n, n), q)
+        return ("e", 0, (4, 4, 5, 5), (2 * n, 2 * n + 1) * 2, q)
 
     def eb(q, n):
-        return ("e", 8, (2, 3), (n, n), q)
-
-    def eb_last(q):
-        return ("e", 8, (2, 2 + core), (core, 1), q)
+        return ("e", 0, (2, 2, 3, 3), (2 * n, 2 * n + 1) * 2, q)
+
+    def eb_all(q):
+        return ("e", 0, (2, 2, 2, 2), (0, 1, 2, 3), q)
+
+    def e_mixed(n):
+        return ("e", 0, (2, 2, 4, 5), (2 * n - 4, 2 * n - 3, n, n), 0)
+
+    def e_part(n):
+        return ("e", 0, (2, 3, 4, 5), (n, n, n, n), 0)
 
     rounds = (
         ((aa(0),), (aa(1),)),
         ((ab(0),),),
         ((ab(1),), (ah(0),), (aa(2), eb(0, 0))),
         ((ab(2),), (ah(1),), (eh(0, 0),)),
-        ((ab(3),), (ah(2),), (aa(3), eb(1, 0)), (eb_last(0),), (eb_last(1),), (eh(1, 0),)),
-        ((eh(0, 1),), (eh(1, 1),), (ah(3),)),
+        ((ab(3),), (ah(2),), (aa(3), eb(1, 0)), (e_mixed(2), e_part(2)), (eb_all(1), eb(1, 1)), (eh(1, 0),)),
+        ((e_mixed(3), e_part(3)), (eh(1, 1),), (ah(3),)),
     )
     units = [unit for group in rounds for unit in group]
 
+    side = [0]
+
     def each(place, action):
-        if len(units[place]) == 1:
-            action(units[place][0])
-        else:
-            for n, unit in enumerate(units[place]):
-                @pl.when(core == n)
-                def _(unit=unit):
-                    action(unit)
+        action(units[place][min(side[0], len(units[place]) - 1)])
 
     def rows_of(block, n, count):
         return held[block, pl.ds(pl.multiple_of(n * count, count), count), :]
@@ -229,8 +232,10 @@
             else:
                 q = unit[4]
                 right = before[pl.ds(q * wide, wide), :]
-                for i, (b, n) in enumerate(zip(blocks, parts)):
-                    value = times(rows_of(b, n, 2 * size), right).reshape(2, 2, NZ, 8, wide)
+                for i in range(2):
+                    chosen = list(zip(blocks, parts))[2 * i : 2 * i + 2]
+                    left = jnp.concatenate([rows_of(b, n, size) for b, n in chosen], axis=0)
+                    value = times(left, right).reshape(2, 2, NZ, 8, wide)
                     for j in range(2):
                         part[place, :, :, pl.ds(8 * j, 8), pl.ds(i * wide, wide)] = value[j]
 
@@ -293,44 +298,54 @@
             else:
                 total = sum_in[place, 0] + sum_in[place, 1]
             for i, (b, n) in enumerate(zip(blocks, parts)):
-                k = base + b % 2 - core
                 if kind == "a":
-                    out[k, pl.ds(pl.multiple_of(8 * n, 8), 8), :] = total[8 * i : 8 * i + 8]
+                    out[base + b % 2 - core, pl.ds(pl.multiple_of(8 * n, 8), 8), :] = total[8 * i : 8 * i + 8]
                 else:
-                    q = unit[4]
-                    out[k, pl.ds(pl.multiple_of(16 * n, 16), 16), pl.ds(q * wide, wide)] = total[:, i * wide : (i + 1) * wide]
+                    q, away = unit[4], 8 if b < 4 else 6
+                    up, over = 8 * (i % 2), wide * (i // 2)
+                    out[away + b % 2 - core, pl.ds(8 * n, 8), pl.ds(q * wide, wide)] = total[up : up + 8, over : over + wide]
 
         each(place, action)
 
     copies = {"a": a_copy, "b": tb_copy, "h": th_copy, "e": e_copy}
-    waited = {kind: 0 for kind in copies}
-
-    def need(kind, count):
-        count *= 1 if kind == "e" else PIECES // PARTS
-        for n in range(waited[kind], count):
-            copies[kind][n].wait_recv()
-        waited[kind] = max(waited[kind], count)
-
-    for kind, n, *rest in plan():
-        if kind == "b":
-            b_copy[n].wait_recv()
-            h_copy[n].start()
-            tb_copy[n].start()
-        elif kind == "h":
-            h_copy[n].wait_recv()
-            th_copy[n].start()
-        elif kind == "unit":
-            for what, count in NEEDS[n]:
-                need(what, count)
-            product(n)
-            for way in range(2):
-                hop(n, way, 0)
-        elif kind == "hop":
-            hop(n, *rest)
-        elif kind == "sum":
-            finish(n)
-        else:
-            put(n)
+
+    def run(needs):
+        waited = {kind: 0 for kind in copies}
+
+        def need(kind, count):
+            count *= 1 if kind == "e" else PIECES // PARTS
+            for n in range(waited[kind], count):
+                copies[kind][n].wait_recv()
+            waited[kind] = max(waited[kind], count)
+
+        for kind, n, *rest in plan(needs):
+            if kind == "b":
+                b_copy[n].wait_recv()
+                h_copy[n].start()
+                tb_copy[n].start()
+            elif kind == "h":
+                h_copy[n].wait_recv()
+                th_copy[n].start()
+            elif kind == "unit":
+                for what, count in needs[n]:
+                    need(what, count)
+                product(n)
+                for way in range(2):
+                    hop(n, way, 0)
+            elif kind == "hop":
+                hop(n, *rest)
+            elif kind == "sum":
+                finish(n)
+            else:
+                put(n)
+        for what, count in (("a", PARTS), ("b", PARTS), ("h", PARTS), ("e", 2)):
+            need(what, count)
+
+    for n in range(2):
+        @pl.when(core == n)
+        def _(n=n):
+            side[0] = n
+            run(NEEDS[n])
 
     remote(held, held, g_send, a_recv.at[0], twin).wait_send()
     steps = sent.at[:, :, pl.ds(1, 3)]

time: 99.2 us -> 99.2 us (level)
  no operation moved by 1% of the time
where the time goes in v5:
time: 99.2 us; the launch traced here: 99 us
  Pallas kernels  96.4 us (97%)
  other arithmetic  1.94 us (2%)
    pallas_call x1, Pallas kernels, local(): pl.pallas_call(kernel, out_shape=jax.ShapeDtypeStruct((9, 32, rows), jnp....  96.4 us

profile of v5, /device:TPU:2, one launch (start us, length us, event | category | flops | bytes accessed | tf_op | source)
XLA Modules:
  0.0 99.0 jit_solution(2915778348856779094)
XLA Ops:
  0.7 96.4 %shard_map.46 = f32[9,32,512]{2,1,0:T(8,128)} custom-call(s32[4,4]{1,0:T(4,128)} %cols.1, f32[1,1]{1,0:T(1,128)} %bitcast.3.threshold, bf16[512,2048]{1,0:T(8,128)(2,1)} %snapshots_in.1, bf16[4,4,128,128]{3,2,1,0:T(8,128)(2,1)} %values_in.1), custom_call_target="tpu_custom_call" | custom-call | tf_op jit(solution)/shard_map/pallas_call | solution.py:368
  97.0 1.9 %multiply_bitcast_fusion = f32[512,9,32]{0,2,1:T(8,128)} fusion(f32[9,32,512]{2,1,0:T(8,128)} %shard_map.46), kind=kLoop, calls=%fused_computation | loop fusion | flops 147456 | bytes 1179648 | tf_op jit(solution)/shard_map/mul | solution.py:397

commit v6 on v4

--- a/solution.py
+++ b/solution.py
@@ -158,7 +158,8 @@
     def portion(block, n):
         return held.at[block, pl.ds(n * (rows // PIECES), rows // PIECES)]
 
-    a_copy = [remote(portion(core, n), portion(core, n), g_send, a_recv.at[n], twin) for n in range(PIECES)]
+    quarters = [held.at[core, pl.ds(n * size, size)] for n in range(PARTS)]
+    a_copy = [remote(quarter, quarter, g_send, a_recv.at[n], twin) for n, quarter in enumerate(quarters)]
     b_copy = [remote(portion(core, n), portion(2 + core, n), g_send, b_recv.at[n], x_down) for n in range(PIECES)]
     e_copy = [
         remote(natural.at[pl.ds(q * wide, wide)], before.at[pl.ds(q * wide, wide)], g_send, e_recv.at[q], x_up)
@@ -220,12 +221,9 @@
             if kind == "a":
                 left = jnp.concatenate([rows_of(b, n, size) for b, n in zip(blocks, parts)], axis=0)
 
-                @pl.loop(0, 2)
-                def _(q):
-                    columns = pl.ds(pl.multiple_of(q * wide, wide), wide)
-                    value = times(left, natural[columns, :]).reshape(2, 2, NZ, 8, wide)
-                    for i in range(2):
-                        part[place, :, :, pl.ds(8 * i, 8), columns] = value[i]
+                value = times(left, natural[...]).reshape(2, 2, NZ, 8, rows)
+                for i in range(2):
+                    part[place, :, :, pl.ds(8 * i, 8), :] = value[i]
             else:
                 q = unit[4]
                 right = before[pl.ds(q * wide, wide), :]
@@ -306,7 +304,7 @@
     waited = {kind: 0 for kind in copies}
 
     def need(kind, count):
-        count *= 1 if kind == "e" else PIECES // PARTS
+        count *= 1 if kind in "ae" else PIECES // PARTS
         for n in range(waited[kind], count):
             copies[kind][n].wait_recv()
         waited[kind] = max(waited[kind], count)
@@ -368,7 +366,7 @@
             pltpu.VMEM((UNITS, 2, 16, rows), jnp.float32),
             dma((2,)),
             dma,
-            *[dma((count,)) for count in (PIECES, PIECES, 2, PIECES, PIECES, PIECES)],
+            *[dma((count,)) for count in (PARTS, PIECES, 2, PIECES, PIECES, PIECES)],
             dma,
             dma,
             dma((UNITS, 2, 4)),

time: 99.2 us -> 98.9 us (level)
  no operation moved by 1% of the time
where the time goes in v6:
time: 98.9 us; the launch traced here: 98.7 us
  Pallas kernels  96.1 us (97%)
  other arithmetic  1.94 us (2%)
    pallas_call x1, Pallas kernels, local(): pl.pallas_call(kernel, out_shape=jax.ShapeDtypeStruct((9, 32, rows), jnp....  96.1 us

profile of v6, /device:TPU:2, one launch (start us, length us, event | category | flops | bytes accessed | tf_op | source)
XLA Modules:
  0.0 98.7 jit_solution(2374668384415801533)
XLA Ops:
  0.7 96.1 %shard_map.46 = f32[9,32,512]{2,1,0:T(8,128)} custom-call(s32[4,4]{1,0:T(4,128)} %cols.1, f32[1,1]{1,0:T(1,128)} %bitcast.3.threshold, bf16[512,2048]{1,0:T(8,128)(2,1)} %snapshots_in.1, bf16[4,4,128,128]{3,2,1,0:T(8,128)(2,1)} %values_in.1), custom_call_target="tpu_custom_call" | custom-call | tf_op jit(solution)/shard_map/pallas_call | solution.py:351
  96.7 1.9 %multiply_bitcast_fusion = f32[512,9,32]{0,2,1:T(8,128)} fusion(f32[9,32,512]{2,1,0:T(8,128)} %shard_map.46), kind=kLoop, calls=%fused_computation | loop fusion | flops 147456 | bytes 1179648 | tf_op jit(solution)/shard_map/mul | solution.py:380
